TPU v7x, 32 devices: a whole 2x2x4 slice. The times are simulated.
32 devices in a mesh: row: 4 (over z), col: 8 (over y, x, core).
Axes of the slice: x: 2, y: 2, z: 4, core: 2. Of those that a mesh axis runs over, the one named last changes fastest.
Arguments:
- grad_first: float32 [4096, 20480], P('row', 'col'), may hold values from -1000 to 1000
- grad_second: float32 [4096, 20480], P('row', 'col'), may hold values from -1000 to 1000
Outputs:
- update: float32 [4096, 20480], P('row', 'col')
All inputs are finite; a program needn't handle non-finite values.
Results may differ from a plain program's by a relative error of at most 0.00014.
Values sent between devices are 32-bit elements; how exact they have to be, the bound alone decides.
A program may use at most 128 MiB of HBM per device.

v0:
```python
import functools

import jax
import jax.numpy as jnp
from jax import lax
from jax.experimental import pallas as pl
from jax.experimental.pallas import tpu as pltpu
from jax.sharding import PartitionSpec as P

BLOCK = 256
HALF = 128
PACKED = BLOCK + 8
ITERS = 6
damping = 0.001
VMEM_LIMIT = 56 * 1024 * 1024


def split(value):
    high = value.astype(jnp.bfloat16)
    low = (value - high.astype(jnp.float32)).astype(jnp.bfloat16)
    return high, low


def dot(left, right, dims=(((1,), (0,)), ((), ()))):
    return lax.dot_general(left, right, dims, preferred_element_type=jnp.float32)


def product(left, right):
    return dot(
        jnp.concatenate([left[0], left[0], left[1]], axis=1),
        jnp.concatenate([right[0], right[1], right[0]], axis=0),
    )


def indices():
    rows = lax.broadcasted_iota(jnp.int32, (HALF, HALF), 0)
    cols = lax.broadcasted_iota(jnp.int32, (HALF, HALF), 1)
    return rows, cols


def pack(write, block):
    rows, cols = indices()
    first, last = block[:HALF, :HALF], block[HALF:, HALF:]
    write(0, HALF, block[:HALF, HALF:])
    write(HALF, HALF, jnp.where(rows <= cols, first, last))
    diagonal = jnp.sum(jnp.where(rows == cols, last, 0.0), axis=0, keepdims=True)
    write(BLOCK, 8, jnp.broadcast_to(diagonal, (8, HALF)))


def unpack(packed):
    rows, cols = indices()
    off = packed[:HALF]
    tile = packed[HALF:BLOCK]
    turned = tile.T
    first = jnp.where(rows <= cols, tile, turned)
    last = jnp.where(rows > cols, tile, jnp.where(rows < cols, turned, packed[BLOCK : BLOCK + 1]))
    return jnp.concatenate(
        [jnp.concatenate([first, off], axis=1), jnp.concatenate([off.T, last], axis=1)], axis=0
    )


def writer(ref, *lead):
    def write(start, size, value):
        ref[(*lead, pl.ds(start, size), slice(None))] = value

    return write


def left_stat_kernel(g1_ref, g2_ref, out_ref):
    total = None
    for step, ref in enumerate((g1_ref, g2_ref)):
        high, low = split(ref[...])
        both = dot(high, jnp.concatenate([high, low], axis=0), (((1,), (1,)), ((), ())))
        cross = both[:, BLOCK:]
        part = both[:, :BLOCK] + (cross + cross.T)
        total = part if total is None else total + part
        pack(writer(out_ref, step, 0), total)


def right_stat_kernel(g1_ref, g2_ref, out_ref):
    total = None
    for step, ref in enumerate((g1_ref, g2_ref)):
        high, low = split(ref[...])
        both = dot(high.T, jnp.concatenate([high, low], axis=1))
        cross = both[:, BLOCK:]
        part = both[:, :BLOCK] + (cross + cross.T)
        total = part if total is None else total + part
        pack(writer(out_ref, step, 0), total)


def stats(kernel, grads, count, tile, index):
    flops = 8 * grads[0].size * BLOCK
    return pl.pallas_call(
        kernel,
        grid=(count,),
        in_specs=[pl.BlockSpec(tile, index)] * 2,
        out_specs=pl.BlockSpec((2, 1, PACKED, HALF), lambda i: (0, i, 0, 0)),
        out_shape=jax.ShapeDtypeStruct((2, count, PACKED, HALF), jnp.float32),
        compiler_params=pltpu.CompilerParams(vmem_limit_bytes=VMEM_LIMIT),
        cost_estimate=pl.CostEstimate(
            flops=flops, bytes_accessed=8 * grads[0].size, transcendentals=0
        ),
    )(*grads)


def root_kernel(count, scale, stat_ref, out_ref, x_ref, m_ref):
    rows = lax.broadcasted_iota(jnp.int32, (BLOCK, BLOCK), 0)
    cols = lax.broadcasted_iota(jnp.int32, (BLOCK, BLOCK), 1)
    identity = jnp.where(rows == cols, 1.0, 0.0)

    def factor_of(scaled):
        return (5.0 * identity - scaled) / 4.0

    def advance(factor_parts, scaled):
        square = product(factor_parts, factor_parts)
        square_parts = split(square)
        fourth = product(square_parts, square_parts)
        return product(split(fourth), split(scaled))

    for slot in range(count):
        damped = unpack(stat_ref[slot]) * scale + damping * identity
        total = jnp.sum(jnp.sum(damped * damped, axis=0, keepdims=True), axis=1, keepdims=True)
        norm = jnp.sqrt(total)
        scaled = damped / norm
        factor = factor_of(scaled)
        x_ref[slot] = factor * lax.rsqrt(jnp.sqrt(norm))
        m_ref[slot] = advance(split(factor), scaled)

    def step(iteration, carry):
        for slot in range(count):
            scaled = m_ref[slot]
            parts = split(factor_of(scaled))
            x_ref[slot] = product(split(x_ref[slot]), parts)
            m_ref[slot] = advance(parts, scaled)
        return carry

    lax.fori_loop(0, ITERS - 2, step, 0)
    for slot in range(count):
        result = product(split(x_ref[slot]), split(factor_of(m_ref[slot])))
        pack(writer(out_ref, slot), result)


def roots(statistic, scale):
    count = statistic.shape[0]
    return pl.pallas_call(
        functools.partial(root_kernel, count, scale),
        out_shape=jax.ShapeDtypeStruct(statistic.shape, jnp.float32),
        scratch_shapes=[pltpu.VMEM((count, BLOCK, BLOCK), jnp.float32)] * 2,
        compiler_params=pltpu.CompilerParams(vmem_limit_bytes=VMEM_LIMIT),
        cost_estimate=pl.CostEstimate(
            flops=count * 20 * 6 * BLOCK**3, bytes_accessed=2 * statistic.size * 4, transcendentals=0
        ),
    )(statistic)


def left_apply_kernel(g1_ref, g2_ref, l1_ref, l2_ref, high_ref, low_ref):
    for step, (g_ref, l_ref) in enumerate(((g1_ref, l1_ref), (g2_ref, l2_ref))):
        half = product(split(unpack(l_ref[0])), split(g_ref[...]))
        high, low = split(half)
        high_ref[step] = high
        low_ref[step] = low


def left_apply(grads, packed, count):
    rows, cols = grads[0].shape
    tiles = 2 if cols % (2 * HALF) == 0 else 1
    width = cols // tiles
    root_spec = lambda first: pl.BlockSpec((1, PACKED, HALF), lambda b, t: (first + b, 0, 0))
    out_spec = pl.BlockSpec((2, BLOCK, width), lambda b, t: (0, b, t))
    return pl.pallas_call(
        left_apply_kernel,
        grid=(count, tiles),
        in_specs=[pl.BlockSpec((BLOCK, width), lambda b, t: (b, t))] * 2
        + [root_spec(0), root_spec(count)],
        out_specs=[out_spec] * 2,
        out_shape=[jax.ShapeDtypeStruct((2, rows, cols), jnp.bfloat16)] * 2,
        compiler_params=pltpu.CompilerParams(vmem_limit_bytes=VMEM_LIMIT),
        cost_estimate=pl.CostEstimate(
            flops=12 * rows * cols * BLOCK, bytes_accessed=16 * rows * cols, transcendentals=0
        ),
    )(*grads, packed, packed)


def right_apply_kernel(high_ref, low_ref, r1_ref, r2_ref, out_ref):
    lefts, rights = [], []
    for step, r_ref in enumerate((r1_ref, r2_ref)):
        high, low = split(unpack(r_ref[0]))
        lefts += [high_ref[step], high_ref[step], low_ref[step]]
        rights += [high, low, high]
    out_ref[...] = dot(jnp.concatenate(lefts, axis=1), jnp.concatenate(rights, axis=0))


def right_apply(high, low, packed, count):
    _, rows, cols = high.shape
    root_spec = lambda first: pl.BlockSpec((1, PACKED, HALF), lambda j: (first + j, 0, 0))
    half_spec = pl.BlockSpec((2, rows, BLOCK), lambda j: (0, 0, j))
    return pl.pallas_call(
        right_apply_kernel,
        grid=(count,),
        in_specs=[half_spec, half_spec, root_spec(0), root_spec(count)],
        out_specs=pl.BlockSpec((rows, BLOCK), lambda j: (0, j)),
        out_shape=jax.ShapeDtypeStruct((rows, cols), jnp.float32),
        compiler_params=pltpu.CompilerParams(vmem_limit_bytes=VMEM_LIMIT),
        cost_estimate=pl.CostEstimate(
            flops=12 * rows * cols * BLOCK, bytes_accessed=12 * rows * cols, transcendentals=0
        ),
    )(high, low, packed, packed)


def scatter(packed, axis):
    devices = lax.axis_size(axis)
    flat = packed.reshape(-1, PACKED, HALF)
    extra = -flat.shape[0] % devices
    if extra:
        flat = jnp.concatenate([flat, jnp.zeros((extra, PACKED, HALF), jnp.float32)], axis=0)
    return lax.psum_scatter(flat, axis, scatter_dimension=0, tiled=True)


def body(grad_first, grad_second):
    grads = (grad_first, grad_second)
    rows, cols = grad_first.shape
    left_count, right_count = rows // BLOCK, cols // BLOCK
    left_scale = 1.0 / (cols * lax.axis_size("col"))
    right_scale = 1.0 / (rows * lax.axis_size("row"))
    left_part = stats(left_stat_kernel, grads, left_count, (BLOCK, cols), lambda i: (i, 0))
    right_part = stats(right_stat_kernel, grads, right_count, (rows, BLOCK), lambda i: (0, i))
    left_sum = scatter(left_part, "col")
    right_sum = scatter(right_part, "row")
    left_roots = lax.all_gather(roots(left_sum, left_scale), "col", axis=0, tiled=True)
    right_own = roots(right_sum, right_scale)
    right_roots = lax.all_gather(right_own, "row", axis=0, tiled=True)
    high, low = left_apply(grads, left_roots, left_count)
    return right_apply(high, low, right_roots, right_count)


def solution(mesh):
    in_specs = (P("row", "col"), P("row", "col"))
    out_specs = P("row", "col")
    return jax.shard_map(body, mesh=mesh, in_specs=in_specs, out_specs=out_specs, check_vma=False)
```

profile of v0, /device:TPU:0, one launch (start us, length us, event | category | flops | bytes accessed | tf_op | source)
XLA Modules:
  0.0 218.9 jit_solution(3310970234850680311)
XLA Ops:
  6.5 0.0 reduce-scatter.7.cloned.1.call-start
  6.5 11.1 %shard_map.28 = f32[2,4,264,128]{3,2,1,0:T(8,128)} custom-call(f32[1024,2560]{1,0:T(8,128)} %g1_ref.5, f32[1024,2560]{1,0:T(8,128)} %g2_ref.5), custom_call_target="tpu_custom_call" | custom-call | flops 5368709120 | bytes 20971520 | tf_op jit(solution)/shard_map/pallas_call | solution.py:93
  17.6 0.0 reduce-scatter.7.cloned.1.call-update
  17.6 0.0 reduce-scatter.9.cloned.1.call-start
  17.7 14.7 %shard_map.31 = f32[2,10,264,128]{3,2,1,0:T(8,128)} custom-call(f32[1024,2560]{1,0:T(8,128)} %g1_ref.5, f32[1024,2560]{1,0:T(8,128)} %g2_ref.5), custom_call_target="tpu_custom_call" | custom-call | flops 5368709120 | bytes 20971520 | tf_op jit(solution)/shard_map/pallas_call | solution.py:93
  32.4 0.0 reduce-scatter.9.cloned.1.call-update
  32.4 0.0 all-gather.3.cloned.1.call-start
  32.4 23.5 %reduce-scatter.7.cloned.1.call-done.stat_ref = f32[1,264,128]{2,1,0:T(8,128)} async-done(((f32[8,264,128]{2,1,0:T(8,128)}), f32[1,264,128]{2,1,0:T(8,128)}) %reduce-scatter.7.cloned.1.call-update) | async-done | bytes 135184
  55.9 6.8 %shard_map.29 = f32[1,264,128]{2,1,0:T(8,128)} custom-call(f32[1,264,128]{2,1,0:T(8,128)} %reduce-scatter.7.cloned.1.call-done.stat_ref), custom_call_target="tpu_custom_call" | custom-call | flops 2013265920 | bytes 270336 | tf_op jit(solution)/shard_map/pallas_call | solution.py:145
  62.7 0.0 all-gather.3.cloned.1.call-update
  62.7 0.2 all-gather.5.cloned.1.call-start
  63.0 49.0 %reduce-scatter.9.cloned.1.call-done.stat_ref = f32[5,264,128]{2,1,0:T(8,128)} async-done(((f32[20,264,128]{2,1,0:T(8,128)}), f32[5,264,128]{2,1,0:T(8,128)}) %reduce-scatter.9.cloned.1.call-update) | async-done | bytes 675856
  112.0 22.4 %shard_map.32 = f32[5,264,128]{2,1,0:T(8,128)} custom-call(f32[5,264,128]{2,1,0:T(8,128)} %reduce-scatter.9.cloned.1.call-done.stat_ref), custom_call_target="tpu_custom_call" | custom-call | flops 10066329600 | bytes 1351680 | tf_op jit(solution)/shard_map/pallas_call | solution.py:145
  134.4 0.0 all-gather.5.cloned.1.call-update
  134.4 2.6 %all-gather.3.cloned.1.call-done.l1_ref.l2_ref = f32[8,264,128]{2,1,0:T(8,128)} async-done(((f32[1,264,128]{2,1,0:T(8,128)}), f32[8,264,128]{2,1,0:T(8,128)}) %all-gather.3.cloned.1.call-update) | async-done | bytes 1081360 | tf_op jit(solution)/shard_map/all_gather | solution.py:229
  137.0 20.8 %shard_map.30 = (bf16[2,1024,2560]{2,1,0:T(8,128)(2,1)}, bf16[2,1024,2560]{2,1,0:T(8,128)(2,1)}) custom-call(f32[1024,2560]{1,0:T(8,128)} %g1_ref.5, f32[1024,2560]{1,0:T(8,128)} %g2_ref.5, f32[8,264,128]{2,1,0:T(8,128)} %all-gather.3.cloned.1.call-done.l1_ref.l2_ref, f32[8,264,128]{2,1,0:T(8,128)} %all-gather.3.cloned.1.call-done.l1_ref.l2_ref), custom_call_target="tpu_custom_call" | custom-call | flops 8053063680 | bytes 41943040 | tf_op jit(solution)/shard_map/pallas_call | solution.py:170
  157.8 36.8 %all-gather.5.cloned.1.call-done.r1_ref.r2_ref = f32[20,264,128]{2,1,0:T(8,128)} async-done(((f32[5,264,128]{2,1,0:T(8,128)}), f32[20,264,128]{2,1,0:T(8,128)}) %all-gather.5.cloned.1.call-update) | async-done | bytes 2703376 | tf_op jit(solution)/shard_map/all_gather | solution.py:231
  194.6 17.8 %shard_map.33 = f32[1024,2560]{1,0:T(8,128)} custom-call(bf16[2,1024,2560]{2,1,0:T(8,128)(2,1)} %get-tuple-element.7.high_ref, bf16[2,1024,2560]{2,1,0:T(8,128)(2,1)} %get-tuple-element.8.low_ref, f32[20,264,128]{2,1,0:T(8,128)} %all-gather.5.cloned.1.call-done.r1_ref.r2_ref, f32[20,264,128]{2,1,0:T(8,128)} %all-gather.5.cloned.1.call-done.r1_ref.r2_ref), custom_call_target="tpu_custom_call" | custom-call | flops 8053063680 | bytes 31457280 | tf_op jit(solution)/shard_map/pallas_call | solution.py:197
Async XLA Ops:
  6.5 49.4 %reduce-scatter.7.cloned.1.call-start = ((), (), s32[]{:S(2)}) async-start(), calls=%async_computation.4 | async-start | bytes 1216512
  17.6 94.3 %reduce-scatter.9.cloned.1.call-start = ((), (), s32[]{:S(2)}) async-start(), calls=%async_computation.5 | async-start | bytes 3379200
  32.4 104.6 %all-gather.3.cloned.1.call-start = ((), (), s32[]{:S(2)}) async-start(), calls=%async_computation.2 | async-start | bytes 1216512 | tf_op jit(solution)/shard_map/all_gather | solution.py:229
  62.7 131.8 %all-gather.5.cloned.1.call-start = ((), (), s32[]{:S(2)}) async-start(), calls=%async_computation.3 | async-start | bytes 3379200 | tf_op jit(solution)/shard_map/all_gather | solution.py:231
Sparse Core Ops, SparseCore 0:
  17.8 38.1 reduce-scatter.6
  58.2 53.6 reduce-scatter.8
  113.8 23.1 all-gather.2
  138.4 56.0 all-gather.4
where the time goes:
time: 220 us; the launch traced here: 219 us
  waiting for transfers between devices  112 us (51%)
  Pallas kernels  93.5 us (42%)
  between operations  13.1 us (6%)
    unnamed x6, waiting for transfers between devices  72.6 us
    all_gather x1, waiting for transfers between devices, body(): right_roots = lax.all_gather(right_own, 'row', axis=0, tiled=True)  36.8 us
    pallas_call x2, Pallas kernels, roots(): pl.pallas_call(functools.partial(root_kernel, count, scale), out_shape=ja...  29.2 us
    pallas_call x2, Pallas kernels, stats(): pl.pallas_call(kernel, grid=(count,), in_specs=[pl.BlockSpec(tile, index)...  25.7 us
    pallas_call x1, Pallas kernels, left_apply(): pl.pallas_call(left_apply_kernel, grid=(count, tiles), in_specs=[pl.Block...  20.8 us
    pallas_call x1, Pallas kernels, right_apply(): pl.pallas_call(right_apply_kernel, grid=(count,), in_specs=[half_spec, ha...  17.8 us
  transfers between devices with their start and end apart: 4, of which 4 were waited for; matrix products, arithmetic and copies ran while one was open for 0% of the time, Pallas kernels for 30%

commit v1 on v0

v1 whole, which is shorter than its diff:
```python
import functools

import jax
import jax.numpy as jnp
from jax import lax
from jax.experimental import pallas as pl
from jax.experimental.pallas import tpu as pltpu
from jax.sharding import PartitionSpec as P

BLOCK = 256
HALF = 128
PACKED = BLOCK + 8
ITERS = 6
damping = 0.001
VMEM_LIMIT = 63 * 1024 * 1024
SLOTS = 3
MESH = pl.DeviceIdType.MESH
NN = (((1,), (0,)), ((), ()))
NT = (((1,), (1,)), ((), ()))


def split(value):
    high = value.astype(jnp.bfloat16)
    low = (value - high.astype(jnp.float32)).astype(jnp.bfloat16)
    return high, low


def dot(left, right, dims=NN):
    return lax.dot_general(left, right, dims, preferred_element_type=jnp.float32)


def product(left, right):
    return dot(
        jnp.concatenate([left[0], left[0], left[1]], axis=1),
        jnp.concatenate([right[0], right[1], right[0]], axis=0),
    )


def indices():
    rows = lax.broadcasted_iota(jnp.int32, (HALF, HALF), 0)
    cols = lax.broadcasted_iota(jnp.int32, (HALF, HALF), 1)
    return rows, cols


def pack(ref, index, block):
    rows, cols = indices()
    first, last = block[:HALF, :HALF], block[HALF:, HALF:]
    ref[index, pl.ds(0, HALF), :] = block[:HALF, HALF:]
    ref[index, pl.ds(HALF, HALF), :] = jnp.where(rows <= cols, first, last)
    diagonal = jnp.sum(jnp.where(rows == cols, last, 0.0), axis=0, keepdims=True)
    ref[index, pl.ds(BLOCK, 8), :] = jnp.broadcast_to(diagonal, (8, HALF))


def unpack(packed):
    rows, cols = indices()
    off = packed[:HALF]
    tile = packed[HALF:BLOCK]
    turned = tile.T
    first = jnp.where(rows <= cols, tile, turned)
    last = jnp.where(rows > cols, tile, jnp.where(rows < cols, turned, packed[BLOCK : BLOCK + 1]))
    return jnp.concatenate(
        [jnp.concatenate([first, off], axis=1), jnp.concatenate([off.T, last], axis=1)], axis=0
    )


def root_of(statistic, scale, x_ref, m_ref):
    rows = lax.broadcasted_iota(jnp.int32, (BLOCK, BLOCK), 0)
    cols = lax.broadcasted_iota(jnp.int32, (BLOCK, BLOCK), 1)
    identity = jnp.where(rows == cols, 1.0, 0.0)

    def factor_of(scaled):
        return (5.0 * identity - scaled) / 4.0

    def advance(factor_parts, scaled):
        square = product(factor_parts, factor_parts)
        square_parts = split(square)
        fourth = product(square_parts, square_parts)
        return product(split(fourth), split(scaled))

    damped = statistic * scale + damping * identity
    total = jnp.sum(jnp.sum(damped * damped, axis=0, keepdims=True), axis=1, keepdims=True)
    norm = jnp.sqrt(total)
    scaled = damped / norm
    factor = factor_of(scaled)
    x_ref[...] = factor * lax.rsqrt(jnp.sqrt(norm))
    m_ref[...] = advance(split(factor), scaled)

    def step(iteration, carry):
        current = m_ref[...]
        parts = split(factor_of(current))
        x_ref[...] = product(split(x_ref[...]), parts)
        m_ref[...] = advance(parts, current)
        return carry

    lax.fori_loop(0, ITERS - 2, step, 0)
    return product(split(x_ref[...]), split(factor_of(m_ref[...])))


def kernel(
    sizes, g1_ref, g2_ref, out_ref, gh, gl, stage, rp, up, dn, rr, lp, lrecv, lr, own, tiles, x_ref, m_ref,
    load_sem, out_sem, up_send, up_recv, dn_send, dn_recv, agu_send, agd_send, ag_recv,
    l_send, l_recv, lag_send, lag_recv,
):
    n, nl, rows, cols = sizes
    lcount, rcount = rows // BLOCK, cols // BLOCK
    M, ML = 2 * rcount, 2 * lcount
    K, KL = pl.cdiv(M, n), pl.cdiv(ML, nl)
    left_scale, right_scale = 1.0 / (cols * nl), 1.0 / (rows * n)
    z, c = lax.axis_index("row"), lax.axis_index("col")
    refs = (g1_ref, g2_ref)

    def load(step, block):
        slot = lax.rem(block, SLOTS)
        columns = pl.ds(pl.multiple_of(block * BLOCK, BLOCK), BLOCK)
        return pltpu.make_async_copy(
            refs[step].at[:, columns], stage.at[step, slot], load_sem.at[step, slot]
        )

    for block in range(min(SLOTS, rcount)):
        for step in range(2):
            load(step, block).start()

    def to_row(source, target, send, recv, row):
        return pltpu.make_async_remote_copy(
            source, target, send, recv, device_id=(row, c), device_id_type=MESH
        )

    def send_up(v, ref):
        return to_row(ref.at[v], up.at[v], up_send.at[v], up_recv.at[v], z + 1)

    def send_down(v, ref):
        return to_row(ref.at[v], dn.at[v], dn_send.at[v], dn_recv.at[v], z - 1)

    def root_up(v):
        return to_row(rr.at[v], rr.at[v], agu_send.at[v], ag_recv.at[v], z + 1)

    def root_down(v):
        return to_row(rr.at[v], rr.at[v], agd_send.at[v], ag_recv.at[v], z - 1)

    def left_out(w):
        return pltpu.make_async_remote_copy(
            lp.at[w], lrecv.at[w // nl, c], l_send.at[w], l_recv.at[w // nl, c],
            device_id=(z, lax.rem(w, nl)), device_id_type=MESH,
        )

    def left_in(kl, source):
        return pltpu.make_async_remote_copy(
            lp.at[0], lrecv.at[kl, source], l_send.at[0], l_recv.at[kl, source],
            device_id=(z, source), device_id_type=MESH,
        )

    def left_root(w, kl, other):
        return pltpu.make_async_remote_copy(
            lr.at[w], lr.at[w], lag_send.at[kl, other], lag_recv.at[w],
            device_id=(z, other), device_id_type=MESH,
        )

    barrier = pltpu.get_barrier_semaphore()

    @pl.when(z > 0)
    def _():
        pl.semaphore_signal(barrier, inc=1, device_id=(z - 1, c), device_id_type=MESH)

    @pl.when(z < n - 1)
    def _():
        pl.semaphore_signal(barrier, inc=1, device_id=(z + 1, c), device_id_type=MESH)

    for d in range(1, nl):
        pl.semaphore_signal(
            barrier, inc=1, device_id=(z, lax.rem(c + d, nl)), device_id_type=MESH
        )
    pl.semaphore_wait(barrier, nl - 1 + jnp.where(z > 0, 1, 0) + jnp.where(z < n - 1, 1, 0))

    def right_stat(block, carry):
        slot = lax.rem(block, SLOTS)
        columns = pl.ds(pl.multiple_of(block * BLOCK, BLOCK), BLOCK)
        total = None
        for step in range(2):
            load(step, block).wait()
            high, low = split(stage[step, slot])
            gh[step, :, columns] = high
            gl[step, :, columns] = low
            turned = high.T
            cross = dot(turned, low)
            part = dot(turned, high) + (cross + cross.T)
            total = part if total is None else total + part
            v = 2 * block + step
            pack(rp, v, total)

        @pl.when(block + SLOTS < rcount)
        def _():
            for step in range(2):
                load(step, block + SLOTS).start()

        for step in range(2):
            v = 2 * block + step
            owner = lax.rem(v, n)

            @pl.when((z == 0) & (owner > 0))
            def _():
                send_up(v, rp).start()

            @pl.when((z == n - 1) & (owner < n - 1))
            def _():
                send_down(v, rp).start()

        return carry

    lax.fori_loop(0, rcount, right_stat, 0)

    def left_stat(block, carry):
        lines = pl.ds(pl.multiple_of(block * BLOCK, BLOCK), BLOCK)
        total = None
        for step in range(2):
            high, low = gh[step, lines, :], gl[step, lines, :]
            cross = dot(high, low, NT)
            part = dot(high, high, NT) + (cross + cross.T)
            total = part if total is None else total + part
            w = 2 * block + step
            pack(lp, w, total)

        for step in range(2):
            w = 2 * block + step

            @pl.when(lax.rem(w, nl) != c)
            def _():
                left_out(w).start()

        return carry

    lax.fori_loop(0, lcount, left_stat, 0)

    def gather(k, d):
        below, above = z - d, z + d

        @pl.when((below >= 0) & (k * n + below < M))
        def _():
            v = k * n + below
            root_up(v).wait_recv()

            @pl.when(z < n - 1)
            def _():
                root_up(v).start()

        @pl.when((above < n) & (k * n + above < M))
        def _():
            v = k * n + above
            root_down(v).wait_recv()

            @pl.when(z > 0)
            def _():
                root_down(v).start()

    def reduce_round(k, slot):
        for d in range(n - 1, 0, -1):
            below, above = z - d, z + d

            @pl.when((above < n) & (z > 0) & (k * n + above < M))
            def _():
                v = k * n + above
                send_up(v, up).wait_recv()
                up[v] = up[v] + rp[v]
                send_up(v, up).start()

            @pl.when((below >= 0) & (z < n - 1) & (k * n + below < M))
            def _():
                v = k * n + below
                send_down(v, dn).wait_recv()
                dn[v] = dn[v] + rp[v]
                send_down(v, dn).start()

        @pl.when(k * n + z < M)
        def _():
            v = k * n + z
            own[slot] = rp[v]

            @pl.when(z > 0)
            def _():
                send_up(v, up).wait_recv()
                own[slot] = own[slot] + up[v]

            @pl.when(z < n - 1)
            def _():
                send_down(v, dn).wait_recv()
                own[slot] = own[slot] + dn[v]

    def left_sum(kl, slot):
        w = kl * nl + c

        @pl.when(w < ML)
        def _():
            own[slot] = lp[w]
            for d in range(1, nl):
                source = lax.rem(c + d, nl)
                left_in(kl, source).wait_recv()
                own[slot] = own[slot] + lrecv[kl, source]

    first_left = max(K - 2, 0)

    def turn(it, carry):
        left = (it >= first_left) & (it < first_left + KL)
        k = jnp.where(it < first_left, it, it - KL)
        kl = it - first_left

        @pl.when(jnp.logical_not(left))
        def _():
            reduce_round(k, it)
            for d in range(1, n):
                @pl.when(k - d >= 0)
                def _():
                    gather(k - d, d)

        @pl.when(left)
        def _():
            left_sum(kl, it)

        exists = jnp.where(left, kl * nl + c < ML, k * n + z < M)

        @pl.when(exists)
        def _():
            scale = jnp.where(left, left_scale, right_scale)
            result = root_of(unpack(own[it]), scale, x_ref, m_ref)
            pack(own, it, result)

            @pl.when(left)
            def _():
                w = kl * nl + c
                lr[w] = own[it]
                for d in range(1, nl):
                    left_root(w, kl, lax.rem(c + d, nl)).start()

            @pl.when(jnp.logical_not(left))
            def _():
                v = k * n + z
                rr[v] = own[it]

                @pl.when(z < n - 1)
                def _():
                    root_up(v).start()

                @pl.when(z > 0)
                def _():
                    root_down(v).start()

        return carry

    lax.fori_loop(0, K + KL, turn, 0)

    def left_arrive(w, carry):
        @pl.when(lax.rem(w, nl) != c)
        def _():
            left_root(w, 0, lax.rem(w, nl)).wait_recv()

        return carry

    lax.fori_loop(0, ML, left_arrive, 0)

    width = cols
    for parts in (2, 3, 5):
        if rcount % parts == 0 and rcount > parts:
            width = cols // parts
            break
    pieces = cols // width

    def left_apply(block, carry):
        lines = pl.ds(pl.multiple_of(block * BLOCK, BLOCK), BLOCK)
        for step in range(2):
            root = split(unpack(lr[2 * block + step]))

            def piece(t, inner):
                columns = pl.ds(pl.multiple_of(t * width, HALF), width)
                high, low = gh[step, lines, columns], gl[step, lines, columns]
                high, low = split(product(root, (high, low)))
                gh[step, lines, columns] = high
                gl[step, lines, columns] = low
                return inner

            lax.fori_loop(0, pieces, piece, 0)

        stage_index = K + block
        for d in range(1, n):
            k = stage_index - d

            @pl.when((k >= 0) & (k < K))
            def _():
                gather(k, d)

        return carry

    lax.fori_loop(0, lcount, left_apply, 0)

    for stage_index in range(K + lcount, K + n - 1):
        for d in range(1, n):
            if 0 <= stage_index - d < K:
                gather(stage_index - d, d)

    def out_copy(block):
        slot = lax.rem(block, 2)
        columns = pl.ds(pl.multiple_of(block * BLOCK, BLOCK), BLOCK)
        return pltpu.make_async_copy(tiles.at[slot], out_ref.at[:, columns], out_sem.at[slot])

    def right_apply(block, carry):
        columns = pl.ds(pl.multiple_of(block * BLOCK, BLOCK), BLOCK)
        slot = lax.rem(block, 2)

        @pl.when(block >= 2)
        def _():
            out_copy(block - 2).wait()

        lefts, rights = [], []
        for step in range(2):
            high, low = split(unpack(rr[2 * block + step]))
            grad_high, grad_low = gh[step, :, columns], gl[step, :, columns]
            lefts += [grad_high, grad_high, grad_low]
            rights += [high, low, high]
        tiles[slot] = dot(jnp.concatenate(lefts, axis=1), jnp.concatenate(rights, axis=0))
        out_copy(block).start()
        return carry

    lax.fori_loop(0, rcount, right_apply, 0)
    for block in range(max(rcount - 2, 0), rcount):
        out_copy(block).wait()

    def drain(v, carry):
        owner = lax.rem(v, n)

        @pl.when((z < n - 1) & (owner > z))
        def _():
            send_up(v, up).wait_send()

        @pl.when((z > 0) & (owner < z))
        def _():
            send_down(v, dn).wait_send()

        @pl.when((z < n - 1) & (owner <= z))
        def _():
            root_up(v).wait_send()

        @pl.when((z > 0) & (owner >= z))
        def _():
            root_down(v).wait_send()

        return carry

    lax.fori_loop(0, M, drain, 0)

    def left_drain(w, carry):
        @pl.when(lax.rem(w, nl) != c)
        def _():
            left_out(w).wait_send()

        @pl.when(lax.rem(w, nl) == c)
        def _():
            for d in range(1, nl):
                left_root(w, w // nl, lax.rem(c + d, nl)).wait_send()

        return carry

    lax.fori_loop(0, ML, left_drain, 0)


def body(n, nl, grad_first, grad_second):
    rows, cols = grad_first.shape
    lcount, rcount = rows // BLOCK, cols // BLOCK
    M, ML = 2 * rcount, 2 * lcount
    K, KL = pl.cdiv(M, n), pl.cdiv(ML, nl)
    f32, bf16 = jnp.float32, jnp.bfloat16
    unit = (PACKED, HALF)
    dma = pltpu.SemaphoreType.DMA
    return pl.pallas_call(
        functools.partial(kernel, (n, nl, rows, cols)),
        in_specs=[pl.BlockSpec(memory_space=pl.ANY)] * 2,
        out_specs=pl.BlockSpec(memory_space=pl.ANY),
        out_shape=jax.ShapeDtypeStruct((rows, cols), f32),
        scratch_shapes=[
            pltpu.VMEM((2, rows, cols), bf16),
            pltpu.VMEM((2, rows, cols), bf16),
            pltpu.VMEM((2, SLOTS, rows, BLOCK), f32),
            pltpu.VMEM((M, *unit), f32),
            pltpu.VMEM((M, *unit), f32),
            pltpu.VMEM((M, *unit), f32),
            pltpu.VMEM((M, *unit), f32),
            pltpu.VMEM((ML, *unit), f32),
            pltpu.VMEM((KL, nl, *unit), f32),
            pltpu.VMEM((ML, *unit), f32),
            pltpu.VMEM((K + KL, *unit), f32),
            pltpu.VMEM((2, rows, BLOCK), f32),
            pltpu.VMEM((BLOCK, BLOCK), f32),
            pltpu.VMEM((BLOCK, BLOCK), f32),
            dma((2, SLOTS)),
            dma((2,)),
            dma((M,)),
            dma((M,)),
            dma((M,)),
            dma((M,)),
            dma((M,)),
            dma((M,)),
            dma((M,)),
            dma((ML,)),
            dma((KL, nl)),
            dma((KL, nl)),
            dma((ML,)),
        ],
        compiler_params=pltpu.CompilerParams(
            collective_id=0, has_side_effects=True, vmem_limit_bytes=VMEM_LIMIT
        ),
    )(grad_first, grad_second)


def solution(mesh):
    spec = P("row", "col")
    return jax.shard_map(
        functools.partial(body, mesh.shape["row"], mesh.shape["col"]),
        mesh=mesh,
        in_specs=(spec, spec),
        out_specs=spec,
        check_vma=False,
    )
```

time: 220 us -> 150 us (0.68)
  waiting for transfers between devices: 112 us -> 0 us
  Pallas kernels: 93.5 us -> 141 us
  between operations: 13.1 us -> 0.01 us
  local copies, waits for them, and re-layouts: 0 us -> 8.78 us
    unnamed x6 -> x0, waiting for transfers between devices: 72.6 us -> none
    pallas_call x6 -> x1, Pallas kernels: 93.5 us -> 141 us  [body(): pl.pallas_call(functools.partial(kernel, (n, nl, rows, cols)), in_specs=[...]
    all_gather x2 -> x0, waiting for transfers between devices: 39.4 us -> none  [the longest x1 36.8 us: body(): right_roots = lax.all_gather(right_own, 'row', axis=0, tiled=True)]
    unnamed x0 -> x1, local copies, waits for them, and re-layouts: none -> 8.78 us
  transfers between devices with their start and end apart: 4 -> 0, of which waited for: 4 -> 0; matrix products, arithmetic and copies ran while one was open for 0% -> 0% of each run, Pallas kernels for 30% -> 0%
where the time goes in v1:
time: 150 us
  Pallas kernels  141 us (94%)
  local copies, waits for them, and re-layouts  8.78 us (6%)
    pallas_call x1, Pallas kernels, body(): pl.pallas_call(functools.partial(kernel, (n, nl, rows, cols)), in_specs=[...  141 us
    unnamed x1, local copies, waits for them, and re-layouts  8.78 us

profile of v1, /device:TPU:0, one launch (start us, length us, event | category | flops | bytes accessed | tf_op | source)
XLA Modules:
  0.0 149.8 jit_solution(1265115552303593575)
XLA Ops:
  0.0 141.0 %shard_map.28 = f32[1024,2560]{1,0:T(8,128)} custom-call(f32[1024,2560]{1,0:T(8,128)} %g1_ref.1, f32[1024,2560]{1,0:T(8,128)} %g2_ref.1), custom_call_target="tpu_custom_call" | custom-call | tf_op jit(solution)/shard_map/pallas_call | solution.py:470
  141.0 8.8 %copy.4 = f32[1024,2560]{1,0:T(8,128)} copy(f32[1024,2560]{1,0:T(8,128)} %shard_map.28) | data formatting | bytes 20971520

commit v2 on v1

--- a/solution.py
+++ b/solution.py
@@ -17,6 +17,111 @@
 MESH = pl.DeviceIdType.MESH
 NN = (((1,), (0,)), ((), ()))
 NT = (((1,), (1,)), ((), ()))
+
+
+NOP, STAT, SEND, LEFT, UP, DOWN, GATHER, ROOT, LAPPLY, RAPPLY = range(10)
+COST = {STAT: 1.15, LEFT: 1.7, ROOT: 5.4, LAPPLY: 1.55, RAPPLY: 1.12}
+START, OVERHEAD, HOP, LINK, SPREAD = 4.0, 0.08, 0.95, 2.785, 11.0
+
+
+def plan(n, rounds, total, left_units, right_blocks, left_blocks):
+    clock = [START] * n
+    line, arrival = {}, {}
+    programs = [[] for _ in range(n)]
+    done = [set() for _ in range(n)]
+    spread = [[None, None] for _ in range(n)]
+
+    def post(source, target, key):
+        end = max(line.get((source, target), 0.0), clock[source]) + LINK
+        line[source, target] = end
+        arrival[key] = end + HOP
+
+    def latest(times):
+        return None if None in times else max(times, default=0.0)
+
+    def choices(z):
+        made = done[z]
+
+        def ready(rank, kind, item, *needs):
+            when = latest(needs)
+            if when is not None and (kind, item) not in made:
+                found.append((when, rank, kind, item))
+
+        def after(kind, item):
+            return 0.0 if (kind, item) in made else None
+
+        found = []
+        for v in range(total):
+            owner = v % n
+            if owner > z > 0:
+                ready(0, UP, v, after(STAT, v // 2), arrival.get((UP, z, v)))
+            if owner < z < n - 1:
+                ready(0, DOWN, v, after(STAT, v // 2), arrival.get((DOWN, z, v)))
+            if owner != z:
+                passed = 0 < z < n - 1
+                ready(1 if passed else 8, GATHER, v, arrival.get((GATHER, z, v)))
+        stats = [j for j in range(right_blocks) if (STAT, j) not in made]
+        for j in stats[:1]:
+            ready(2, STAT, j)
+        if z in (0, n - 1):
+            for k in range(rounds):
+                last = min(k * n + n, total) - 1
+                ready(0, SEND, k, after(STAT, last // 2))
+        if not stats:
+            for b in [b for b in range(left_blocks) if (LEFT, b) not in made][:1]:
+                ready(3, LEFT, b)
+        for k in range(rounds):
+            v = k * n + z
+            if v < total:
+                needs = [after(STAT, v // 2)]
+                needs += [arrival.get((UP, z, v))] if z > 0 else []
+                needs += [arrival.get((DOWN, z, v))] if z < n - 1 else []
+                ready(4, ROOT, k, *needs)
+        ready(4, ROOT, rounds, spread[z][0])
+        for w in [w for w in range(left_units) if (LAPPLY, w) not in made][:1]:
+            ready(5, LAPPLY, w, spread[z][1])
+        if (LAPPLY, left_units - 1) in made:
+            for j in [j for j in range(right_blocks) if (RAPPLY, j) not in made][:1]:
+                needs = [after(ROOT, v // n) if v % n == z else after(GATHER, v) for v in (2 * j, 2 * j + 1)]
+                ready(6, RAPPLY, j, *needs)
+        return found
+
+    while True:
+        options = []
+        for z in range(n):
+            found = choices(z)
+            if found:
+                now = [f for f in found if f[0] <= clock[z] + 0.05]
+                pick = min(now, key=lambda f: (f[1], f[0])) if now else min(found)
+                options.append((max(clock[z], pick[0]), z, pick))
+        if not options:
+            return programs
+        when, z, (_, _, kind, item) = min(options)
+        clock[z] = when + OVERHEAD + COST.get(kind, 0.0)
+        programs[z].append((kind, item))
+        done[z].add((kind, item))
+        if kind == SEND:
+            units = range(item * n, min(item * n + n, total))
+            for v in reversed(units):
+                if z == 0 and v % n > 0:
+                    post(0, 1, (UP, 1, v))
+            for v in units:
+                if z == n - 1 and v % n < n - 1:
+                    post(z, z - 1, (DOWN, z - 1, v))
+        elif kind == LEFT and item == left_blocks - 1:
+            spread[z][0] = clock[z] + SPREAD
+        elif kind == UP:
+            post(z, z + 1, (UP, z + 1, item))
+        elif kind == DOWN:
+            post(z, z - 1, (DOWN, z - 1, item))
+        elif kind == ROOT and item == rounds:
+            spread[z][1] = clock[z] + SPREAD
+        elif kind in (ROOT, GATHER):
+            v = item * n + z if kind == ROOT else item
+            if v % n <= z < n - 1:
+                post(z, z + 1, (GATHER, z + 1, v))
+            if v % n >= z > 0:
+                post(z, z - 1, (GATHER, z - 1, v))
 
 
 def split(value):
@@ -171,9 +276,36 @@
         )
     pl.semaphore_wait(barrier, nl - 1 + jnp.where(z > 0, 1, 0) + jnp.where(z < n - 1, 1, 0))
 
-    def right_stat(block, carry):
+    programs = plan(n, K, M, ML, rcount, lcount)
+    length = max(len(program) for program in programs)
+    base = 16 * max(M, ML, K + KL, rcount)
+    held = max(h for h in (1, 2, 3) if base**h < 2**31)
+    words = []
+    for start in range(0, length, held):
+        values = []
+        for program in programs:
+            part = (program + [(NOP, 0)] * (length + held))[start : start + held]
+            values.append(sum((item * 16 + kind) * base**j for j, (kind, item) in enumerate(part)))
+        word = jnp.int32(values[0])
+        for row in range(1, n):
+            word = jnp.where(z == row, values[row], word)
+        words.append(word)
+
+    def code_at(i):
+        index, place = i // held, lax.rem(i, held)
+        word = words[0]
+        for j in range(1, len(words)):
+            word = jnp.where(index == j, words[j], word)
+        for j in range(1, held):
+            word = jnp.where(place >= j, word // base, word)
+        return lax.rem(word, base)
+
+    def columns_of(block):
+        return pl.ds(pl.multiple_of(block * BLOCK, BLOCK), BLOCK)
+
+    def right_stat(block):
         slot = lax.rem(block, SLOTS)
-        columns = pl.ds(pl.multiple_of(block * BLOCK, BLOCK), BLOCK)
+        columns = columns_of(block)
         total = None
         for step in range(2):
             load(step, block).wait()
@@ -184,40 +316,34 @@
             cross = dot(turned, low)
             part = dot(turned, high) + (cross + cross.T)
             total = part if total is None else total + part
-            v = 2 * block + step
-            pack(rp, v, total)
+            pack(rp, 2 * block + step, total)
 
         @pl.when(block + SLOTS < rcount)
         def _():
             for step in range(2):
                 load(step, block + SLOTS).start()
 
-        for step in range(2):
-            v = 2 * block + step
-            owner = lax.rem(v, n)
-
-            @pl.when((z == 0) & (owner > 0))
-            def _():
-                send_up(v, rp).start()
-
-            @pl.when((z == n - 1) & (owner < n - 1))
-            def _():
-                send_down(v, rp).start()
-
-        return carry
-
-    lax.fori_loop(0, rcount, right_stat, 0)
-
-    def left_stat(block, carry):
-        lines = pl.ds(pl.multiple_of(block * BLOCK, BLOCK), BLOCK)
+    def send_round(k):
+        for d in range(1, n):
+            up_unit, down_unit = k * n + n - d, k * n + d - 1
+
+            @pl.when((z == 0) & (up_unit < M))
+            def _():
+                send_up(up_unit, rp).start()
+
+            @pl.when((z == n - 1) & (down_unit < M))
+            def _():
+                send_down(down_unit, rp).start()
+
+    def left_stat(block):
+        lines = columns_of(block)
         total = None
         for step in range(2):
             high, low = gh[step, lines, :], gl[step, lines, :]
             cross = dot(high, low, NT)
             part = dot(high, high, NT) + (cross + cross.T)
             total = part if total is None else total + part
-            w = 2 * block + step
-            pack(lp, w, total)
+            pack(lp, 2 * block + step, total)
 
         for step in range(2):
             w = 2 * block + step
@@ -226,113 +352,76 @@
             def _():
                 left_out(w).start()
 
-        return carry
-
-    lax.fori_loop(0, lcount, left_stat, 0)
-
-    def gather(k, d):
-        below, above = z - d, z + d
-
-        @pl.when((below >= 0) & (k * n + below < M))
-        def _():
-            v = k * n + below
+    def relay_up(v):
+        send_up(v, up).wait_recv()
+        up[v] = up[v] + rp[v]
+        send_up(v, up).start()
+
+    def relay_down(v):
+        send_down(v, dn).wait_recv()
+        dn[v] = dn[v] + rp[v]
+        send_down(v, dn).start()
+
+    def gather(v):
+        owner = lax.rem(v, n)
+
+        @pl.when(owner < z)
+        def _():
             root_up(v).wait_recv()
 
             @pl.when(z < n - 1)
             def _():
                 root_up(v).start()
 
-        @pl.when((above < n) & (k * n + above < M))
-        def _():
-            v = k * n + above
+        @pl.when(owner > z)
+        def _():
             root_down(v).wait_recv()
 
             @pl.when(z > 0)
             def _():
                 root_down(v).start()
 
-    def reduce_round(k, slot):
-        for d in range(n - 1, 0, -1):
-            below, above = z - d, z + d
-
-            @pl.when((above < n) & (z > 0) & (k * n + above < M))
-            def _():
-                v = k * n + above
+    def root(k):
+        left = k >= K
+        kl = k - K
+        v, w = k * n + z, kl * nl + c
+
+        @pl.when(jnp.logical_not(left))
+        def _():
+            own[...] = rp[v]
+
+            @pl.when(z > 0)
+            def _():
                 send_up(v, up).wait_recv()
-                up[v] = up[v] + rp[v]
-                send_up(v, up).start()
-
-            @pl.when((below >= 0) & (z < n - 1) & (k * n + below < M))
-            def _():
-                v = k * n + below
+                own[...] = own[...] + up[v]
+
+            @pl.when(z < n - 1)
+            def _():
                 send_down(v, dn).wait_recv()
-                dn[v] = dn[v] + rp[v]
-                send_down(v, dn).start()
-
-        @pl.when(k * n + z < M)
-        def _():
-            v = k * n + z
-            own[slot] = rp[v]
-
-            @pl.when(z > 0)
-            def _():
-                send_up(v, up).wait_recv()
-                own[slot] = own[slot] + up[v]
-
-            @pl.when(z < n - 1)
-            def _():
-                send_down(v, dn).wait_recv()
-                own[slot] = own[slot] + dn[v]
-
-    def left_sum(kl, slot):
-        w = kl * nl + c
-
-        @pl.when(w < ML)
-        def _():
-            own[slot] = lp[w]
+                own[...] = own[...] + dn[v]
+
+        @pl.when(left & (w < ML))
+        def _():
+            own[...] = lp[w]
             for d in range(1, nl):
                 source = lax.rem(c + d, nl)
                 left_in(kl, source).wait_recv()
-                own[slot] = own[slot] + lrecv[kl, source]
-
-    first_left = max(K - 2, 0)
-
-    def turn(it, carry):
-        left = (it >= first_left) & (it < first_left + KL)
-        k = jnp.where(it < first_left, it, it - KL)
-        kl = it - first_left
-
-        @pl.when(jnp.logical_not(left))
-        def _():
-            reduce_round(k, it)
-            for d in range(1, n):
-                @pl.when(k - d >= 0)
-                def _():
-                    gather(k - d, d)
-
-        @pl.when(left)
-        def _():
-            left_sum(kl, it)
-
-        exists = jnp.where(left, kl * nl + c < ML, k * n + z < M)
-
-        @pl.when(exists)
+                own[...] = own[...] + lrecv[kl, source]
+
+        @pl.when(jnp.logical_not(left) | (w < ML))
         def _():
             scale = jnp.where(left, left_scale, right_scale)
-            result = root_of(unpack(own[it]), scale, x_ref, m_ref)
-            pack(own, it, result)
+            result = root_of(unpack(own[...]), scale, x_ref, m_ref)
 
             @pl.when(left)
             def _():
-                w = kl * nl + c
-                lr[w] = own[it]
+                pack(lr, w, result)
                 for d in range(1, nl):
                     left_root(w, kl, lax.rem(c + d, nl)).start()
 
             @pl.when(jnp.logical_not(left))
             def _():
-                v = k * n + z
-                rr[v] = own[it]
+                pack(rr, v, result)
 
                 @pl.when(z < n - 1)
                 def _():
@@ -341,19 +430,6 @@
                 @pl.when(z > 0)
                 def _():
                     root_down(v).start()
-
-        return carry
-
-    lax.fori_loop(0, K + KL, turn, 0)
-
-    def left_arrive(w, carry):
-        @pl.when(lax.rem(w, nl) != c)
-        def _():
-            left_root(w, 0, lax.rem(w, nl)).wait_recv()
-
-        return carry
-
-    lax.fori_loop(0, ML, left_arrive, 0)
 
     width = cols
     for parts in (2, 3, 5):
@@ -362,45 +438,33 @@
             break
     pieces = cols // width
 
-    def left_apply(block, carry):
-        lines = pl.ds(pl.multiple_of(block * BLOCK, BLOCK), BLOCK)
-        for step in range(2):
-            root = split(unpack(lr[2 * block + step]))
-
-            def piece(t, inner):
-                columns = pl.ds(pl.multiple_of(t * width, HALF), width)
-                high, low = gh[step, lines, columns], gl[step, lines, columns]
-                high, low = split(product(root, (high, low)))
-                gh[step, lines, columns] = high
-                gl[step, lines, columns] = low
-                return inner
-
-            lax.fori_loop(0, pieces, piece, 0)
-
-        stage_index = K + block
-        for d in range(1, n):
-            k = stage_index - d
-
-            @pl.when((k >= 0) & (k < K))
-            def _():
-                gather(k, d)
-
-        return carry
-
-    lax.fori_loop(0, lcount, left_apply, 0)
-
-    for stage_index in range(K + lcount, K + n - 1):
-        for d in range(1, n):
-            if 0 <= stage_index - d < K:
-                gather(stage_index - d, d)
+    def left_apply(w):
+        @pl.when(lax.rem(w, nl) != c)
+        def _():
+            left_root(w, 0, lax.rem(w, nl)).wait_recv()
+
+        step = lax.rem(w, 2)
+        lines = columns_of(w // 2)
+        factor = split(unpack(lr[w]))
+
+        def piece(t, inner):
+            columns = pl.ds(pl.multiple_of(t * width, HALF), width)
+            high, low = gh[step, lines, columns], gl[step, lines, columns]
+            high, low = split(product(factor, (high, low)))
+            gh[step, lines, columns] = high
+            gl[step, lines, columns] = low
+            return inner
+
+        lax.fori_loop(0, pieces, piece, 0)
 
     def out_copy(block):
         slot = lax.rem(block, 2)
-        columns = pl.ds(pl.multiple_of(block * BLOCK, BLOCK), BLOCK)
-        return pltpu.make_async_copy(tiles.at[slot], out_ref.at[:, columns], out_sem.at[slot])
-
-    def right_apply(block, carry):
-        columns = pl.ds(pl.multiple_of(block * BLOCK, BLOCK), BLOCK)
+        return pltpu.make_async_copy(
+            tiles.at[slot], out_ref.at[:, columns_of(block)], out_sem.at[slot]
+        )
+
+    def right_apply(block):
+        columns = columns_of(block)
         slot = lax.rem(block, 2)
 
         @pl.when(block >= 2)
@@ -415,9 +479,23 @@
             rights += [high, low, high]
         tiles[slot] = dot(jnp.concatenate(lefts, axis=1), jnp.concatenate(rights, axis=0))
         out_copy(block).start()
+
+    work = {
+        STAT: right_stat, SEND: send_round, LEFT: left_stat, UP: relay_up, DOWN: relay_down,
+        GATHER: gather, ROOT: root, LAPPLY: left_apply, RAPPLY: right_apply,
+    }
+
+    def turn(i, carry):
+        code = code_at(i)
+        kind, item = lax.rem(code, 16), code // 16
+        for name, act in work.items():
+            @pl.when(kind == name)
+            def _():
+                act(item)
+
         return carry
 
-    lax.fori_loop(0, rcount, right_apply, 0)
+    lax.fori_loop(0, length, turn, 0)
     for block in range(max(rcount - 2, 0), rcount):
         out_copy(block).wait()
 
@@ -483,7 +561,7 @@
             pltpu.VMEM((ML, *unit), f32),
             pltpu.VMEM((KL, nl, *unit), f32),
             pltpu.VMEM((ML, *unit), f32),
-            pltpu.VMEM((K + KL, *unit), f32),
+            pltpu.VMEM(unit, f32),
             pltpu.VMEM((2, rows, BLOCK), f32),
             pltpu.VMEM((BLOCK, BLOCK), f32),
             pltpu.VMEM((BLOCK, BLOCK), f32),

time: 150 us -> 105 us (0.70)
  Pallas kernels: 141 us -> 95.7 us
    pallas_call x1, Pallas kernels: 141 us -> 95.7 us  [body(): pl.pallas_call(functools.partial(kernel, (n, nl, rows, cols)), in_specs=[...]
where the time goes in v2:
time: 105 us
  Pallas kernels  95.7 us (91%)
  local copies, waits for them, and re-layouts  8.78 us (8%)
    pallas_call x1, Pallas kernels, body(): pl.pallas_call(functools.partial(kernel, (n, nl, rows, cols)), in_specs=[...  95.7 us
    unnamed x1, local copies, waits for them, and re-layouts  8.78 us

profile of v2, /device:TPU:0, one launch (start us, length us, event | category | flops | bytes accessed | tf_op | source)
XLA Modules:
  0.0 104.5 jit_solution(1477330417563277179)
XLA Ops:
  0.0 95.7 %shard_map.28 = f32[1024,2560]{1,0:T(8,128)} custom-call(f32[1024,2560]{1,0:T(8,128)} %g1_ref.1, f32[1024,2560]{1,0:T(8,128)} %g2_ref.1), custom_call_target="tpu_custom_call" | custom-call | tf_op jit(solution)/shard_map/pallas_call | solution.py:548
  95.7 8.8 %copy.4 = f32[1024,2560]{1,0:T(8,128)} copy(f32[1024,2560]{1,0:T(8,128)} %shard_map.28) | data formatting | bytes 20971520

commit v3 on v2

--- a/solution.py
+++ b/solution.py
@@ -12,7 +12,7 @@
 PACKED = BLOCK + 8
 ITERS = 6
 damping = 0.001
-VMEM_LIMIT = 63 * 1024 * 1024
+VMEM_LIMIT = 50 * 1024 * 1024
 SLOTS = 3
 MESH = pl.DeviceIdType.MESH
 NN = (((1,), (0,)), ((), ()))
@@ -21,14 +21,15 @@
 
 NOP, STAT, SEND, LEFT, UP, DOWN, GATHER, ROOT, LAPPLY, RAPPLY = range(10)
 COST = {STAT: 1.15, LEFT: 1.7, ROOT: 5.4, LAPPLY: 1.55, RAPPLY: 1.12}
-START, OVERHEAD, HOP, LINK, SPREAD = 4.0, 0.08, 0.95, 2.785, 11.0
+START, OVERHEAD, HOP, LINK, SPREAD = 2.0, 0.07, 0.95, 2.785, 11.0
+FIRST = 2
 
 
 def plan(n, rounds, total, left_units, right_blocks, left_blocks):
-    clock = [START] * n
+    clock = [START + FIRST * COST[STAT]] * n
     line, arrival = {}, {}
     programs = [[] for _ in range(n)]
-    done = [set() for _ in range(n)]
+    done = [{(STAT, j) for j in range(FIRST)} for _ in range(n)]
     spread = [[None, None] for _ in range(n)]
 
     def post(source, target, key):
@@ -57,9 +58,8 @@
                 ready(0, UP, v, after(STAT, v // 2), arrival.get((UP, z, v)))
             if owner < z < n - 1:
                 ready(0, DOWN, v, after(STAT, v // 2), arrival.get((DOWN, z, v)))
-            if owner != z:
-                passed = 0 < z < n - 1
-                ready(1 if passed else 8, GATHER, v, arrival.get((GATHER, z, v)))
+            if owner != z and 0 < z < n - 1:
+                ready(1, GATHER, v, arrival.get((GATHER, z, v)))
         stats = [j for j in range(right_blocks) if (STAT, j) not in made]
         for j in stats[:1]:
             ready(2, STAT, j)
@@ -82,7 +82,14 @@
             ready(5, LAPPLY, w, spread[z][1])
         if (LAPPLY, left_units - 1) in made:
             for j in [j for j in range(right_blocks) if (RAPPLY, j) not in made][:1]:
-                needs = [after(ROOT, v // n) if v % n == z else after(GATHER, v) for v in (2 * j, 2 * j + 1)]
+                needs = []
+                for v in (2 * j, 2 * j + 1):
+                    if v % n == z:
+                        needs.append(after(ROOT, v // n))
+                    elif 0 < z < n - 1:
+                        needs.append(after(GATHER, v))
+                    else:
+                        needs.append(arrival.get((GATHER, z, v)))
                 ready(6, RAPPLY, j, *needs)
         return found
 
@@ -202,8 +209,8 @@
 
 
 def kernel(
-    sizes, g1_ref, g2_ref, out_ref, gh, gl, stage, rp, up, dn, rr, lp, lrecv, lr, own, tiles, x_ref, m_ref,
-    load_sem, out_sem, up_send, up_recv, dn_send, dn_recv, agu_send, agd_send, ag_recv,
+    sizes, g1_ref, g2_ref, out_ref, gh, gl, stage, rp, up, dn, rr, lp, lrecv, lr, own, x_ref, m_ref,
+    load_sem, up_send, up_recv, dn_send, dn_recv, agu_send, agd_send, ag_recv,
     l_send, l_recv, lag_send, lag_recv,
 ):
     n, nl, rows, cols = sizes
@@ -231,32 +238,32 @@
         )
 
     def send_up(v, ref):
-        return to_row(ref.at[v], up.at[v], up_send.at[v], up_recv.at[v], z + 1)
+        return to_row(ref.at[v], up.at[v], up_send, up_recv.at[v], z + 1)
 
     def send_down(v, ref):
-        return to_row(ref.at[v], dn.at[v], dn_send.at[v], dn_recv.at[v], z - 1)
+        return to_row(ref.at[v], dn.at[v], dn_send, dn_recv.at[v], z - 1)
 
     def root_up(v):
-        return to_row(rr.at[v], rr.at[v], agu_send.at[v], ag_recv.at[v], z + 1)
+        return to_row(rr.at[v], rr.at[v], agu_send, ag_recv.at[v], z + 1)
 
     def root_down(v):
-        return to_row(rr.at[v], rr.at[v], agd_send.at[v], ag_recv.at[v], z - 1)
+        return to_row(rr.at[v], rr.at[v], agd_send, ag_recv.at[v], z - 1)
 
     def left_out(w):
         return pltpu.make_async_remote_copy(
-            lp.at[w], lrecv.at[w // nl, c], l_send.at[w], l_recv.at[w // nl, c],
+            lp.at[w], lrecv.at[w // nl, c], l_send, l_recv.at[w // nl, c],
             device_id=(z, lax.rem(w, nl)), device_id_type=MESH,
         )
 
     def left_in(kl, source):
         return pltpu.make_async_remote_copy(
-            lp.at[0], lrecv.at[kl, source], l_send.at[0], l_recv.at[kl, source],
+            lp.at[0], lrecv.at[kl, source], l_send, l_recv.at[kl, source],
             device_id=(z, source), device_id_type=MESH,
         )
 
     def left_root(w, kl, other):
         return pltpu.make_async_remote_copy(
-            lr.at[w], lr.at[w], lag_send.at[kl, other], lag_recv.at[w],
+            lr.at[w], lr.at[w], lag_send, lag_recv.at[w],
             device_id=(z, other), device_id_type=MESH,
         )
 
@@ -274,32 +281,6 @@
         pl.semaphore_signal(
             barrier, inc=1, device_id=(z, lax.rem(c + d, nl)), device_id_type=MESH
         )
-    pl.semaphore_wait(barrier, nl - 1 + jnp.where(z > 0, 1, 0) + jnp.where(z < n - 1, 1, 0))
-
-    programs = plan(n, K, M, ML, rcount, lcount)
-    length = max(len(program) for program in programs)
-    base = 16 * max(M, ML, K + KL, rcount)
-    held = max(h for h in (1, 2, 3) if base**h < 2**31)
-    words = []
-    for start in range(0, length, held):
-        values = []
-        for program in programs:
-            part = (program + [(NOP, 0)] * (length + held))[start : start + held]
-            values.append(sum((item * 16 + kind) * base**j for j, (kind, item) in enumerate(part)))
-        word = jnp.int32(values[0])
-        for row in range(1, n):
-            word = jnp.where(z == row, values[row], word)
-        words.append(word)
-
-    def code_at(i):
-        index, place = i // held, lax.rem(i, held)
-        word = words[0]
-        for j in range(1, len(words)):
-            word = jnp.where(index == j, words[j], word)
-        for j in range(1, held):
-            word = jnp.where(place >= j, word // base, word)
-        return lax.rem(word, base)
-
     def columns_of(block):
         return pl.ds(pl.multiple_of(block * BLOCK, BLOCK), BLOCK)
 
@@ -323,6 +304,13 @@
             for step in range(2):
                 load(step, block + SLOTS).start()
 
+    def first_stat(block, carry):
+        right_stat(block)
+        return carry
+
+    lax.fori_loop(0, FIRST, first_stat, 0)
+    pl.semaphore_wait(barrier, nl - 1 + jnp.where(z > 0, 1, 0) + jnp.where(z < n - 1, 1, 0))
+
     def send_round(k):
         for d in range(1, n):
             up_unit, down_unit = k * n + n - d, k * n + d - 1
@@ -381,6 +369,11 @@
             def _():
                 root_down(v).start()
 
+    def arrive(v):
+        @pl.when(((z == 0) | (z == n - 1)) & (lax.rem(v, n) != z))
+        def _():
+            gather(v)
+
     def root(k):
         left = k >= K
         kl = k - K
@@ -457,84 +450,121 @@
 
         lax.fori_loop(0, pieces, piece, 0)
 
-    def out_copy(block):
-        slot = lax.rem(block, 2)
-        return pltpu.make_async_copy(
-            tiles.at[slot], out_ref.at[:, columns_of(block)], out_sem.at[slot]
-        )
-
     def right_apply(block):
         columns = columns_of(block)
-        slot = lax.rem(block, 2)
-
-        @pl.when(block >= 2)
-        def _():
-            out_copy(block - 2).wait()
-
+        arrive(2 * block)
+        arrive(2 * block + 1)
         lefts, rights = [], []
         for step in range(2):
             high, low = split(unpack(rr[2 * block + step]))
             grad_high, grad_low = gh[step, :, columns], gl[step, :, columns]
             lefts += [grad_high, grad_high, grad_low]
             rights += [high, low, high]
-        tiles[slot] = dot(jnp.concatenate(lefts, axis=1), jnp.concatenate(rights, axis=0))
-        out_copy(block).start()
+        out_ref[:, columns] = dot(jnp.concatenate(lefts, axis=1), jnp.concatenate(rights, axis=0))
 
     work = {
         STAT: right_stat, SEND: send_round, LEFT: left_stat, UP: relay_up, DOWN: relay_down,
         GATHER: gather, ROOT: root, LAPPLY: left_apply, RAPPLY: right_apply,
     }
-
-    def turn(i, carry):
-        code = code_at(i)
-        kind, item = lax.rem(code, 16), code // 16
-        for name, act in work.items():
-            @pl.when(kind == name)
-            def _():
-                act(item)
-
+    programs = plan(n, K, M, ML, rcount, lcount)
+    digit = 16
+    while digit < 16 * max(M, ML, K + KL, rcount):
+        digit *= 2
+    held = max(h for h in (1, 2, 3) if digit**h < 2**31)
+    lists = []
+    for program in programs:
+        program = program + [(NOP, 0)] * (-len(program) % held)
+        codes = [item * 16 + kind for kind, item in program]
+        lists.append(
+            [sum(code * digit**j for j, code in enumerate(codes[i : i + held])) for i in range(0, len(codes), held)]
+        )
+
+    def of_row(values):
+        value = jnp.int32(values[0])
+        for row in range(1, n):
+            value = jnp.where(z == row, values[row], value)
+        return value
+
+    longest = max(len(words) for words in lists)
+    words = [of_row([w[i] if i < len(w) else 0 for w in lists]) for i in range(longest)]
+    last = of_row([len(w) for w in lists])
+
+    def look_up(values, index, width):
+        if len(values) == 1:
+            return values[0]
+        half = width // 2
+        low = look_up(values[:half], index, half)
+        if len(values) <= half:
+            return low
+        return jnp.where(lax.rem(index, width) >= half, look_up(values[half:], index, half), low)
+
+    def choose(kind, names):
+        if len(names) == 1:
+            return work[names[0]]
+        middle = (len(names) + 1) // 2
+        low, high = choose(kind, names[:middle]), choose(kind, names[middle:])
+
+        def act(item):
+            @pl.when(kind < names[middle])
+            def _():
+                low(item)
+
+            @pl.when(kind >= names[middle])
+            def _():
+                high(item)
+
+        return act
+
+    def turn(index, carry):
+        width = 1
+        while width < longest:
+            width *= 2
+
+        def task(j, word):
+            code = lax.rem(word, digit)
+            kind, item = lax.rem(code, 16), lax.div(code, 16)
+
+            @pl.when(kind != NOP)
+            def _():
+                choose(kind, sorted(work))(item)
+
+            return lax.div(word, digit)
+
+        lax.fori_loop(0, held, task, look_up(words, index, width))
         return carry
 
-    lax.fori_loop(0, length, turn, 0)
-    for block in range(max(rcount - 2, 0), rcount):
-        out_copy(block).wait()
-
-    def drain(v, carry):
-        owner = lax.rem(v, n)
-
-        @pl.when((z < n - 1) & (owner > z))
-        def _():
-            send_up(v, up).wait_send()
-
-        @pl.when((z > 0) & (owner < z))
-        def _():
-            send_down(v, dn).wait_send()
-
-        @pl.when((z < n - 1) & (owner <= z))
-        def _():
-            root_up(v).wait_send()
-
-        @pl.when((z > 0) & (owner >= z))
-        def _():
-            root_down(v).wait_send()
-
-        return carry
-
-    lax.fori_loop(0, M, drain, 0)
-
-    def left_drain(w, carry):
-        @pl.when(lax.rem(w, nl) != c)
-        def _():
-            left_out(w).wait_send()
-
-        @pl.when(lax.rem(w, nl) == c)
-        def _():
-            for d in range(1, nl):
-                left_root(w, w // nl, lax.rem(c + d, nl)).wait_send()
-
-        return carry
-
-    lax.fori_loop(0, ML, left_drain, 0)
+    lax.fori_loop(0, last, turn, 0)
+
+    def sent(ref, sem, count):
+        if count:
+            whole = ref.at[pl.ds(0, count)]
+            to_row(whole, whole, sem, ag_recv.at[0], z).wait_send()
+
+    for row in range(n):
+        @pl.when(z == row)
+        def _():
+            owners = [v % n for v in range(M)]
+            if row < n - 1:
+                sent(up, up_send, sum(owner > row for owner in owners))
+                sent(rr, agu_send, sum(owner <= row for owner in owners))
+            if row > 0:
+                sent(dn, dn_send, sum(owner < row for owner in owners))
+                sent(rr, agd_send, sum(owner >= row for owner in owners))
+
+    def left_sent(own_count):
+        sent(lp, l_send, ML - own_count)
+        sent(lrecv.at[0], lag_send, own_count * (nl - 1))
+
+    if ML % nl:
+        @pl.when(c < ML % nl)
+        def _():
+            left_sent(ML // nl + 1)
+
+        @pl.when(c >= ML % nl)
+        def _():
+            left_sent(ML // nl)
+    else:
+        left_sent(ML // nl)
 
 
 def body(n, nl, grad_first, grad_second):
@@ -548,8 +578,8 @@
     return pl.pallas_call(
         functools.partial(kernel, (n, nl, rows, cols)),
         in_specs=[pl.BlockSpec(memory_space=pl.ANY)] * 2,
-        out_specs=pl.BlockSpec(memory_space=pl.ANY),
-        out_shape=jax.ShapeDtypeStruct((rows, cols), f32),
+        out_specs=pl.BlockSpec(memory_space=pltpu.VMEM),
+        out_shape=pltpu.VMEM((rows, cols), f32),
         scratch_shapes=[
             pltpu.VMEM((2, rows, cols), bf16),
             pltpu.VMEM((2, rows, cols), bf16),
@@ -562,21 +592,19 @@
             pltpu.VMEM((KL, nl, *unit), f32),
             pltpu.VMEM((ML, *unit), f32),
             pltpu.VMEM(unit, f32),
-            pltpu.VMEM((2, rows, BLOCK), f32),
             pltpu.VMEM((BLOCK, BLOCK), f32),
             pltpu.VMEM((BLOCK, BLOCK), f32),
             dma((2, SLOTS)),
-            dma((2,)),
+            dma,
             dma((M,)),
+            dma,
             dma((M,)),
+            dma,
+            dma,
             dma((M,)),
-            dma((M,)),
-            dma((M,)),
-            dma((M,)),
-            dma((M,)),
-            dma((ML,)),
+            dma,
             dma((KL, nl)),
-            dma((KL, nl)),
+            dma,
             dma((ML,)),
         ],
         compiler_params=pltpu.CompilerParams(

time: 105 us -> 95.7 us (0.911)
  local copies, waits for them, and re-layouts: 8.78 us -> 4.09 us
  Pallas kernels: 95.7 us -> 91.1 us
    unnamed x1, local copies, waits for them, and re-layouts: 8.78 us -> 4.09 us
    pallas_call x1, Pallas kernels: 95.7 us -> 91.1 us  [body(): pl.pallas_call(functools.partial(kernel, (n, nl, rows, cols)), in_specs=[...]
where the time goes in v3:
time: 95.7 us; the launch traced here: 95.2 us
  Pallas kernels  91.1 us (95%)
  local copies, waits for them, and re-layouts  4.09 us (4%)
    pallas_call x1, Pallas kernels, body(): pl.pallas_call(functools.partial(kernel, (n, nl, rows, cols)), in_specs=[...  91.1 us
    unnamed x1, local copies, waits for them, and re-layouts  4.09 us

profile of v3, /device:TPU:0, one launch (start us, length us, event | category | flops | bytes accessed | tf_op | source)
XLA Modules:
  0.0 95.2 jit_solution(2520580615202640338)
XLA Ops:
  0.0 91.1 %shard_map.28 = f32[1024,2560]{1,0:T(8,128)S(1)} custom-call(f32[1024,2560]{1,0:T(8,128)} %g1_ref.1, f32[1024,2560]{1,0:T(8,128)} %g2_ref.1), custom_call_target="tpu_custom_call" | custom-call | tf_op jit(solution)/shard_map/pallas_call | solution.py:578
  91.1 4.1 %copy.4 = f32[1024,2560]{1,0:T(8,128)} copy(f32[1024,2560]{1,0:T(8,128)S(1)} %shard_map.28) | data formatting | bytes 20971520

commit v4 on v3

--- a/solution.py
+++ b/solution.py
@@ -19,23 +19,32 @@
 NT = (((1,), (1,)), ((), ()))
 
 
-NOP, STAT, SEND, LEFT, UP, DOWN, GATHER, ROOT, LAPPLY, RAPPLY = range(10)
-COST = {STAT: 1.15, LEFT: 1.7, ROOT: 5.4, LAPPLY: 1.55, RAPPLY: 1.12}
-START, OVERHEAD, HOP, LINK, SPREAD = 2.0, 0.07, 0.95, 2.785, 11.0
-FIRST = 2
-
-
-def plan(n, rounds, total, left_units, right_blocks, left_blocks):
+NOP, STAT, SEND, LEFT, UP, DOWN, GATHER, OPEN, STEPS, ROOT, OPEN2, STEPS2, ROOT2, LAPPLY, RAPPLY = range(15)
+COST = {
+    STAT: 1.12, LEFT: 1.72, OPEN: 1.6, STEPS: 1.6, ROOT: 0.8, OPEN2: 2.1, STEPS2: 2.15, ROOT2: 1.1, LAPPLY: 1.52, RAPPLY: 1.14,
+}
+START, OVERHEAD, HOP, LINK, SPREAD = 2.3, 0.06, 3.0, 2.785, 9.0
+FIRST, SEGMENTS = 2, 2
+
+
+def plan(n, rounds, total, left_units, right_blocks, left_blocks, groups):
     clock = [START + FIRST * COST[STAT]] * n
     line, arrival = {}, {}
     programs = [[] for _ in range(n)]
     done = [{(STAT, j) for j in range(FIRST)} for _ in range(n)]
     spread = [[None, None] for _ in range(n)]
+    opened = [[] for _ in range(n)]
 
     def post(source, target, key):
         end = max(line.get((source, target), 0.0), clock[source]) + LINK
         line[source, target] = end
         arrival[key] = end + HOP
+
+    def pass_on(z, v):
+        if v % n <= z < n - 1:
+            post(z, z + 1, (GATHER, z + 1, v))
+        if v % n >= z > 0:
+            post(z, z - 1, (GATHER, z - 1, v))
 
     def latest(times):
         return None if None in times else max(times, default=0.0)
@@ -70,14 +79,33 @@
         if not stats:
             for b in [b for b in range(left_blocks) if (LEFT, b) not in made][:1]:
                 ready(3, LEFT, b)
-        for k in range(rounds):
-            v = k * n + z
-            if v < total:
-                needs = [after(STAT, v // 2)]
-                needs += [arrival.get((UP, z, v))] if z > 0 else []
-                needs += [arrival.get((DOWN, z, v))] if z < n - 1 else []
-                ready(4, ROOT, k, *needs)
-        ready(4, ROOT, rounds, spread[z][0])
+        def closed(group):
+            return after(ROOT if len(group) == 1 else ROOT2, group) == 0.0
+
+        for group in groups:
+            needs = []
+            for k in group:
+                v = k * n + z
+                if k == rounds:
+                    needs.append(spread[z][0])
+                elif v < total:
+                    needs.append(after(STAT, v // 2))
+                    needs += [arrival.get((UP, z, v))] if z > 0 else []
+                    needs += [arrival.get((DOWN, z, v))] if z < n - 1 else []
+            if all(closed(other) for other in opened[z]):
+                ready(4, OPEN if len(group) == 1 else OPEN2, group, *needs)
+        for group in opened[z]:
+            if not closed(group):
+                middle, end = (STEPS, ROOT) if len(group) == 1 else (STEPS2, ROOT2)
+                steps = [i for i in range(SEGMENTS) if (middle, (i, group)) not in made]
+                for i in steps[:1]:
+                    ready(3.5, middle, (i, group))
+                if not steps:
+                    ready(3.5, end, group)
+
+        def rooted(k):
+            return 0.0 if any(k in group and closed(group) for group in groups) else None
+
         for w in [w for w in range(left_units) if (LAPPLY, w) not in made][:1]:
             ready(5, LAPPLY, w, spread[z][1])
         if (LAPPLY, left_units - 1) in made:
@@ -85,7 +113,7 @@
                 needs = []
                 for v in (2 * j, 2 * j + 1):
                     if v % n == z:
-                        needs.append(after(ROOT, v // n))
+                        needs.append(rooted(v // n))
                     elif 0 < z < n - 1:
                         needs.append(after(GATHER, v))
                     else:
@@ -105,8 +133,18 @@
             return programs
         when, z, (_, _, kind, item) = min(options)
         clock[z] = when + OVERHEAD + COST.get(kind, 0.0)
-        programs[z].append((kind, item))
         done[z].add((kind, item))
+        if kind in (OPEN, OPEN2):
+            opened[z].append(item)
+        pairs = [group for group in groups if len(group) == 2]
+        number = item
+        if kind in (OPEN, ROOT):
+            number = item[0]
+        elif kind in (OPEN2, ROOT2):
+            number = pairs.index(item)
+        elif kind in (STEPS, STEPS2):
+            number = 0
+        programs[z].append((kind, number))
         if kind == SEND:
             units = range(item * n, min(item * n + n, total))
             for v in reversed(units):
@@ -121,14 +159,14 @@
             post(z, z + 1, (UP, z + 1, item))
         elif kind == DOWN:
             post(z, z - 1, (DOWN, z - 1, item))
-        elif kind == ROOT and item == rounds:
-            spread[z][1] = clock[z] + SPREAD
-        elif kind in (ROOT, GATHER):
-            v = item * n + z if kind == ROOT else item
-            if v % n <= z < n - 1:
-                post(z, z + 1, (GATHER, z + 1, v))
-            if v % n >= z > 0:
-                post(z, z - 1, (GATHER, z - 1, v))
+        elif kind == GATHER:
+            pass_on(z, item)
+        elif kind in (ROOT, ROOT2):
+            for k in item:
+                if k == rounds:
+                    spread[z][1] = clock[z] + SPREAD
+                elif k * n + z < total:
+                    pass_on(z, k * n + z)
 
 
 def split(value):
@@ -175,37 +213,52 @@
     )
 
 
-def root_of(statistic, scale, x_ref, m_ref):
+def groups_of(rounds):
+    return [(k,) for k in range(rounds - 2)] + [(rounds,), (rounds - 2,), (rounds - 1,)] if rounds > 3 else [(k,) for k in range(rounds + 1)]
+
+
+def factor_of(scaled):
     rows = lax.broadcasted_iota(jnp.int32, (BLOCK, BLOCK), 0)
     cols = lax.broadcasted_iota(jnp.int32, (BLOCK, BLOCK), 1)
-    identity = jnp.where(rows == cols, 1.0, 0.0)
-
-    def factor_of(scaled):
-        return (5.0 * identity - scaled) / 4.0
-
-    def advance(factor_parts, scaled):
-        square = product(factor_parts, factor_parts)
-        square_parts = split(square)
-        fourth = product(square_parts, square_parts)
-        return product(split(fourth), split(scaled))
-
-    damped = statistic * scale + damping * identity
-    total = jnp.sum(jnp.sum(damped * damped, axis=0, keepdims=True), axis=1, keepdims=True)
-    norm = jnp.sqrt(total)
-    scaled = damped / norm
-    factor = factor_of(scaled)
-    x_ref[...] = factor * lax.rsqrt(jnp.sqrt(norm))
-    m_ref[...] = advance(split(factor), scaled)
-
+    return jnp.where(rows == cols, 1.25, 0.0) - scaled * 0.25
+
+
+def advance_all(parts, scaled):
+    squares = [split(product(p, p)) for p in parts]
+    fourths = [product(p, p) for p in squares]
+    return [product(split(f), split(m)) for f, m in zip(fourths, scaled)]
+
+
+def root_open(statistics, scales, x_ref, m_ref):
+    rows = lax.broadcasted_iota(jnp.int32, (BLOCK, BLOCK), 0)
+    cols = lax.broadcasted_iota(jnp.int32, (BLOCK, BLOCK), 1)
+    scaled, factors = [], []
+    for i, (statistic, scale) in enumerate(zip(statistics, scales)):
+        damped = statistic * scale + jnp.where(rows == cols, damping, 0.0)
+        total = jnp.sum(jnp.sum(damped * damped, axis=0, keepdims=True), axis=1, keepdims=True)
+        norm = jnp.sqrt(total)
+        scaled.append(damped / norm)
+        factors.append(factor_of(scaled[i]))
+        x_ref[i] = factors[i] * lax.rsqrt(jnp.sqrt(norm))
+    for i, value in enumerate(advance_all([split(f) for f in factors], scaled)):
+        m_ref[i] = value
+
+
+def root_steps(chains, count, x_ref, m_ref):
     def step(iteration, carry):
-        current = m_ref[...]
-        parts = split(factor_of(current))
-        x_ref[...] = product(split(x_ref[...]), parts)
-        m_ref[...] = advance(parts, current)
+        scaled = [m_ref[i] for i in range(chains)]
+        parts = [split(factor_of(m)) for m in scaled]
+        for i in range(chains):
+            x_ref[i] = product(split(x_ref[i]), parts[i])
+        for i, value in enumerate(advance_all(parts, scaled)):
+            m_ref[i] = value
         return carry
 
-    lax.fori_loop(0, ITERS - 2, step, 0)
-    return product(split(x_ref[...]), split(factor_of(m_ref[...])))
+    lax.fori_loop(0, count, step, 0)
+
+
+def root_close(chains, x_ref, m_ref):
+    return [product(split(x_ref[i]), split(factor_of(m_ref[i]))) for i in range(chains)]
 
 
 def kernel(
@@ -220,6 +273,8 @@
     left_scale, right_scale = 1.0 / (cols * nl), 1.0 / (rows * n)
     z, c = lax.axis_index("row"), lax.axis_index("col")
     refs = (g1_ref, g2_ref)
+    groups = groups_of(K)
+    pairs = [group for group in groups if len(group) == 2]
 
     def load(step, block):
         slot = lax.rem(block, SLOTS)
@@ -374,55 +429,92 @@
         def _():
             gather(v)
 
-    def root(k):
+    def collect(k, slot):
         left = k >= K
         kl = k - K
         v, w = k * n + z, kl * nl + c
 
-        @pl.when(jnp.logical_not(left))
-        def _():
-            own[...] = rp[v]
+        @pl.when(jnp.logical_not(left) & (v < M))
+        def _():
+            own[slot] = rp[v]
 
             @pl.when(z > 0)
             def _():
                 send_up(v, up).wait_recv()
-                own[...] = own[...] + up[v]
+                own[slot] = own[slot] + up[v]
 
             @pl.when(z < n - 1)
             def _():
                 send_down(v, dn).wait_recv()
-                own[...] = own[...] + dn[v]
+                own[slot] = own[slot] + dn[v]
 
         @pl.when(left & (w < ML))
         def _():
-            own[...] = lp[w]
+            own[slot] = lp[w]
             for d in range(1, nl):
                 source = lax.rem(c + d, nl)
                 left_in(kl, source).wait_recv()
-                own[...] = own[...] + lrecv[kl, source]
-
-        @pl.when(jnp.logical_not(left) | (w < ML))
-        def _():
-            scale = jnp.where(left, left_scale, right_scale)
-            result = root_of(unpack(own[...]), scale, x_ref, m_ref)
-
-            @pl.when(left)
-            def _():
-                pack(lr, w, result)
-                for d in range(1, nl):
-                    left_root(w, kl, lax.rem(c + d, nl)).start()
-
-            @pl.when(jnp.logical_not(left))
-            def _():
-                pack(rr, v, result)
-
-                @pl.when(z < n - 1)
-                def _():
-                    root_up(v).start()
-
-                @pl.when(z > 0)
-                def _():
-                    root_down(v).start()
+                own[slot] = own[slot] + lrecv[kl, source]
+
+    def scale_of(k):
+        return jnp.where(k >= K, left_scale, right_scale)
+
+    def deliver(k, result):
+        left = k >= K
+        kl = k - K
+        v, w = k * n + z, kl * nl + c
+
+        @pl.when(left & (w < ML))
+        def _():
+            pack(lr, w, result)
+            for d in range(1, nl):
+                left_root(w, kl, lax.rem(c + d, nl)).start()
+
+        @pl.when(jnp.logical_not(left) & (v < M))
+        def _():
+            pack(rr, v, result)
+
+            @pl.when(z < n - 1)
+            def _():
+                root_up(v).start()
+
+            @pl.when(z > 0)
+            def _():
+                root_down(v).start()
+
+    def members(item):
+        first, second = jnp.int32(pairs[0][0]), jnp.int32(pairs[0][1])
+        for j in range(1, len(pairs)):
+            first = jnp.where(item == j, pairs[j][0], first)
+            second = jnp.where(item == j, pairs[j][1], second)
+        return first, second
+
+    def opening(ks):
+        for slot, k in enumerate(ks):
+            collect(k, slot)
+        root_open([unpack(own[slot]) for slot in range(len(ks))], [scale_of(k) for k in ks], x_ref, m_ref)
+
+    def closing(ks):
+        for k, result in zip(ks, root_close(len(ks), x_ref, m_ref)):
+            deliver(k, result)
+
+    def open_one(k):
+        opening((k,))
+
+    def steps_one(item):
+        root_steps(1, (ITERS - 2) // SEGMENTS, x_ref, m_ref)
+
+    def close_one(k):
+        closing((k,))
+
+    def open_two(item):
+        opening(members(item))
+
+    def steps_two(item):
+        root_steps(2, (ITERS - 2) // SEGMENTS, x_ref, m_ref)
+
+    def close_two(item):
+        closing(members(item))
 
     width = cols
     for parts in (2, 3, 5):
@@ -464,9 +556,11 @@
 
     work = {
         STAT: right_stat, SEND: send_round, LEFT: left_stat, UP: relay_up, DOWN: relay_down,
-        GATHER: gather, ROOT: root, LAPPLY: left_apply, RAPPLY: right_apply,
+        GATHER: gather, OPEN: open_one, STEPS: steps_one, ROOT: close_one,
+        OPEN2: open_two, STEPS2: steps_two, ROOT2: close_two, LAPPLY: left_apply, RAPPLY: right_apply,
     }
-    programs = plan(n, K, M, ML, rcount, lcount)
+    programs = plan(n, K, M, ML, rcount, lcount, groups)
+    used = sorted({kind for program in programs for kind, _ in program} & set(work))
     digit = 16
     while digit < 16 * max(M, ML, K + KL, rcount):
         digit *= 2
@@ -526,7 +620,7 @@
 
             @pl.when(kind != NOP)
             def _():
-                choose(kind, sorted(work))(item)
+                choose(kind, used)(item)
 
             return lax.div(word, digit)
 
@@ -591,9 +685,9 @@
             pltpu.VMEM((ML, *unit), f32),
             pltpu.VMEM((KL, nl, *unit), f32),
             pltpu.VMEM((ML, *unit), f32),
-            pltpu.VMEM(unit, f32),
-            pltpu.VMEM((BLOCK, BLOCK), f32),
-            pltpu.VMEM((BLOCK, BLOCK), f32),
+            pltpu.VMEM((2, *unit), f32),
+            pltpu.VMEM((2, BLOCK, BLOCK), f32),
+            pltpu.VMEM((2, BLOCK, BLOCK), f32),
             dma((2, SLOTS)),
             dma,
             dma((M,)),

time: 95.7 us -> 92 us (0.961)
  Pallas kernels: 91.1 us -> 87.8 us
    pallas_call x1, Pallas kernels: 91.1 us -> 87.8 us  [body(): pl.pallas_call(functools.partial(kernel, (n, nl, rows, cols)), in_specs=[...]
where the time goes in v4:
time: 92 us; the launch traced here: 91.9 us
  Pallas kernels  87.8 us (95%)
  local copies, waits for them, and re-layouts  4.09 us (4%)
    pallas_call x1, Pallas kernels, body(): pl.pallas_call(functools.partial(kernel, (n, nl, rows, cols)), in_specs=[...  87.8 us
    unnamed x1, local copies, waits for them, and re-layouts  4.09 us

profile of v4, /device:TPU:0, one launch (start us, length us, event | category | flops | bytes accessed | tf_op | source)
XLA Modules:
  0.0 91.9 jit_solution(5269867765260479042)
XLA Ops:
  0.0 87.8 %shard_map.28 = f32[1024,2560]{1,0:T(8,128)S(1)} custom-call(f32[1024,2560]{1,0:T(8,128)} %g1_ref.1, f32[1024,2560]{1,0:T(8,128)} %g2_ref.1), custom_call_target="tpu_custom_call" | custom-call | tf_op jit(solution)/shard_map/pallas_call | solution.py:672
  87.8 4.1 %copy.4 = f32[1024,2560]{1,0:T(8,128)} copy(f32[1024,2560]{1,0:T(8,128)S(1)} %shard_map.28) | data formatting | bytes 20971520

commit v5 on v4

--- a/solution.py
+++ b/solution.py
@@ -25,6 +25,7 @@
 }
 START, OVERHEAD, HOP, LINK, SPREAD = 2.3, 0.06, 3.0, 2.785, 9.0
 FIRST, SEGMENTS = 2, 2
+MARGIN = 3.0
 
 
 def plan(n, rounds, total, left_units, right_blocks, left_blocks, groups):
@@ -79,6 +80,9 @@
         if not stats:
             for b in [b for b in range(left_blocks) if (LEFT, b) not in made][:1]:
                 ready(3, LEFT, b)
+        def late(when):
+            return when if when is None or 0 < z < n - 1 else when + MARGIN
+
         def closed(group):
             return after(ROOT if len(group) == 1 else ROOT2, group) == 0.0
 
@@ -90,8 +94,8 @@
                     needs.append(spread[z][0])
                 elif v < total:
                     needs.append(after(STAT, v // 2))
-                    needs += [arrival.get((UP, z, v))] if z > 0 else []
-                    needs += [arrival.get((DOWN, z, v))] if z < n - 1 else []
+                    needs += [late(arrival.get((UP, z, v)))] if z > 0 else []
+                    needs += [late(arrival.get((DOWN, z, v)))] if z < n - 1 else []
             if all(closed(other) for other in opened[z]):
                 ready(4, OPEN if len(group) == 1 else OPEN2, group, *needs)
         for group in opened[z]:
@@ -254,7 +258,8 @@
             m_ref[i] = value
         return carry
 
-    lax.fori_loop(0, count, step, 0)
+    for iteration in range(count):
+        step(iteration, 0)
 
 
 def root_close(chains, x_ref, m_ref):
@@ -516,12 +521,7 @@
     def close_two(item):
         closing(members(item))
 
-    width = cols
-    for parts in (2, 3, 5):
-        if rcount % parts == 0 and rcount > parts:
-            width = cols // parts
-            break
-    pieces = cols // width
+    width, pieces = cols, 1
 
     def left_apply(w):
         @pl.when(lax.rem(w, nl) != c)

time: 92 us -> 91.2 us (level)
  Pallas kernels: 87.8 us -> 86.8 us
    pallas_call x1, Pallas kernels: 87.8 us -> 86.8 us  [body(): pl.pallas_call(functools.partial(kernel, (n, nl, rows, cols)), in_specs=[...]
where the time goes in v5:
time: 91.2 us; the launch traced here: 90.9 us
  Pallas kernels  86.8 us (95%)
  local copies, waits for them, and re-layouts  4.09 us (4%)
    pallas_call x1, Pallas kernels, body(): pl.pallas_call(functools.partial(kernel, (n, nl, rows, cols)), in_specs=[...  86.8 us
    unnamed x1, local copies, waits for them, and re-layouts  4.09 us

profile of v5, /device:TPU:0, one launch (start us, length us, event | category | flops | bytes accessed | tf_op | source)
XLA Modules:
  0.0 90.9 jit_solution(13565935352366049232)
XLA Ops:
  0.0 86.8 %shard_map.28 = f32[1024,2560]{1,0:T(8,128)S(1)} custom-call(f32[1024,2560]{1,0:T(8,128)} %g1_ref.1, f32[1024,2560]{1,0:T(8,128)} %g2_ref.1), custom_call_target="tpu_custom_call" | custom-call | tf_op jit(solution)/shard_map/pallas_call | solution.py:672
  86.8 4.1 %copy.4 = f32[1024,2560]{1,0:T(8,128)} copy(f32[1024,2560]{1,0:T(8,128)S(1)} %shard_map.28) | data formatting | bytes 20971520

commit v6 on v5

--- a/solution.py
+++ b/solution.py
@@ -561,6 +561,7 @@
     }
     programs = plan(n, K, M, ML, rcount, lcount, groups)
     used = sorted({kind for program in programs for kind, _ in program} & set(work))
+    weight = {name: sum(kind == name for p in programs for kind, _ in p) for name in used}
     digit = 16
     while digit < 16 * max(M, ML, K + KL, rcount):
         digit *= 2
@@ -595,7 +596,10 @@
     def choose(kind, names):
         if len(names) == 1:
             return work[names[0]]
-        middle = (len(names) + 1) // 2
+        weights = [weight[name] for name in names]
+        middle = min(
+            range(1, len(names)), key=lambda m: abs(sum(weights[:m]) - sum(weights[m:]))
+        )
         low, high = choose(kind, names[:middle]), choose(kind, names[middle:])
 
         def act(item):

time: 91.2 us -> 91.2 us (level)
  no operation moved by 1% of the time
where the time goes in v6:
time: 91.2 us; the launch traced here: 90.9 us
  Pallas kernels  86.8 us (95%)
  local copies, waits for them, and re-layouts  4.09 us (4%)
    pallas_call x1, Pallas kernels, body(): pl.pallas_call(functools.partial(kernel, (n, nl, rows, cols)), in_specs=[...  86.8 us
    unnamed x1, local copies, waits for them, and re-layouts  4.09 us

profile of v6, /device:TPU:0, one launch (start us, length us, event | category | flops | bytes accessed | tf_op | source)
XLA Modules:
  0.0 90.9 jit_solution(2506070230051876689)
XLA Ops:
  0.0 86.8 %shard_map.28 = f32[1024,2560]{1,0:T(8,128)S(1)} custom-call(f32[1024,2560]{1,0:T(8,128)} %g1_ref.1, f32[1024,2560]{1,0:T(8,128)} %g2_ref.1), custom_call_target="tpu_custom_call" | custom-call | tf_op jit(solution)/shard_map/pallas_call | solution.py:676
  86.8 4.1 %copy.4 = f32[1024,2560]{1,0:T(8,128)} copy(f32[1024,2560]{1,0:T(8,128)S(1)} %shard_map.28) | data formatting | bytes 20971520
